TPU v7x, 256 devices: a whole 4x4x8 slice. The times are simulated.
256 devices in a mesh: seq: 4 (over x_lo, core), dp: 64 (over x_hi, y, z).
Axes of the slice: x: 4 (x_hi: 2, x_lo: 2; x = x_hi * 2 + x_lo), y: 4, z: 8, core: 2. Of those that a mesh axis runs over, the one named last changes fastest.
Arguments:
- residual: bfloat16 [49152, 2560], P(('seq', 'dp')), may hold values from -6 to 6
- query_raw: bfloat16 [49152, 2560], P(('seq', 'dp')), may hold values from -60 to 60
- key_raw: bfloat16 [49152, 2560], P(('seq', 'dp')), may hold values from -60 to 60
- values: bfloat16 [49152, 2560], P(('seq', 'dp')), may hold values from -6 to 6
- residual_grad: bfloat16 [49152, 2560], P(('seq', 'dp')), may hold values from -6 to 6
- modulated_grad: bfloat16 [49152, 2560], P(('seq', 'dp')), may hold values from -24 to 24
- condition: float32 [64, 2, 2560], P('dp'), may hold values from -3 to 3
- modulation: float32 [2, 2560], P(None, ('seq', 'dp')), may hold values from -0.5 to 0.5
- norm_gains: float32 [2, 2560], P(None, ('seq', 'dp')), may hold values from 0.25 to 1.75
Outputs:
- input_grad: bfloat16 [49152, 2560], P(('seq', 'dp'))
- query_grad: bfloat16 [49152, 2560], P(('seq', 'dp'))
- key_grad: bfloat16 [49152, 2560], P(('seq', 'dp'))
- value_grad: bfloat16 [49152, 2560], P(('seq', 'dp'))
- param_grads: float32 [5, 2560], P(None, ('seq', 'dp'))
All inputs are finite; a program needn't handle non-finite values.
Results may differ from a plain program's by a relative error of at most 0.009.
The roundings to bfloat16 on the way count: a program that leaves them out, or rounds other values in their place, can miss the bound.
Values may be sent and summed in bfloat16 or wider, within the bound.
A program may use at most 128 MiB of HBM per device.

v0:
```python
import jax
import jax.numpy as jnp
from jax import lax
from jax.sharding import PartitionSpec as P

HEAD_DIM = 128
epsilon = 1e-06


def root_scale(raw_values):
    floats = raw_values.astype(jnp.float32)
    return lax.rsqrt(jnp.mean(floats * floats, axis=1, keepdims=True) + epsilon)


def head_scores(query_head, key_head):
    return lax.dot_general(
        query_head, key_head, (((1,), (1,)), ((), ())), preferred_element_type=jnp.float32
    ) * query_head.shape[-1] ** (-0.5)


def head_forward(pieces):
    query_head, key_head, value_head = pieces
    scores = head_scores(query_head, key_head)
    row_max = jnp.max(scores, axis=1, keepdims=True)
    row_sum = jnp.sum(jnp.exp(scores - row_max), axis=1, keepdims=True)
    logsum = row_max + jnp.log(row_sum)
    weights_low = jnp.exp(scores - logsum).astype(jnp.bfloat16)
    attended = jnp.dot(weights_low, value_head, preferred_element_type=jnp.float32).astype(
        jnp.bfloat16
    )
    return (attended, logsum[:, 0])


def head_backward(pieces):
    query_head, key_head, value_head, attended, attended_grad, logsum = pieces
    scores = head_scores(query_head, key_head)
    weights = jnp.exp(scores - logsum[:, None])
    row_dot = jnp.sum(
        attended_grad.astype(jnp.float32) * attended.astype(jnp.float32), axis=1, keepdims=True
    )
    weight_grad = lax.dot_general(
        attended_grad, value_head, (((1,), (1,)), ((), ())), preferred_element_type=jnp.float32
    )
    score_grad = (weights * (weight_grad - row_dot) * query_head.shape[-1] ** (-0.5)).astype(
        jnp.bfloat16
    )
    value_part = lax.dot_general(
        weights.astype(jnp.bfloat16),
        attended_grad,
        (((0,), (0,)), ((), ())),
        preferred_element_type=jnp.float32,
    )
    query_part = jnp.dot(score_grad, key_head, preferred_element_type=jnp.float32)
    key_part = lax.dot_general(
        score_grad, query_head, (((0,), (0,)), ((), ())), preferred_element_type=jnp.float32
    )
    return (query_part, key_part, value_part)


def stream_pass(residual, attended, modulated, residual_grad, modulated_grad):
    gate_row = modulated[0]
    scale_row = modulated[1]
    summed = residual.astype(jnp.float32) + gate_row * attended.astype(jnp.float32)
    centered = summed - jnp.mean(summed, axis=1, keepdims=True)
    norm_scale = lax.rsqrt(jnp.mean(centered * centered, axis=1, keepdims=True) + epsilon)
    normed = centered * norm_scale
    scaled_grad = modulated_grad.astype(jnp.float32) * (1.0 + scale_row)
    stream_grad = residual_grad.astype(jnp.float32) + norm_scale * (
        scaled_grad
        - jnp.mean(scaled_grad, axis=1, keepdims=True)
        - normed * jnp.mean(scaled_grad * normed, axis=1, keepdims=True)
    )
    attended_grad = (stream_grad * gate_row).astype(jnp.bfloat16)
    return (stream_grad, normed, attended_grad)


def norm_backward(raw_values, inverse, gain_row, upstream):
    floats = raw_values.astype(jnp.float32)
    weighted = gain_row * upstream
    return (
        inverse * weighted
        - floats * inverse**3 * jnp.mean(floats * weighted, axis=1, keepdims=True)
    ).astype(jnp.bfloat16)


def partial_sums(
    attended,
    stream_grad,
    normed,
    modulated_grad,
    query_raw,
    query_scale,
    query_part,
    key_raw,
    key_scale,
    key_part,
):
    grad_floats = modulated_grad.astype(jnp.float32)
    return jnp.stack(
        [
            jnp.sum(stream_grad * attended.astype(jnp.float32), axis=0),
            jnp.sum(grad_floats, axis=0),
            jnp.sum(grad_floats * normed, axis=0),
            jnp.sum(query_part * query_raw.astype(jnp.float32) * query_scale, axis=0),
            jnp.sum(key_part * key_raw.astype(jnp.float32) * key_scale, axis=0),
        ]
    )


def per_device(
    residual,
    query_raw,
    key_raw,
    values,
    residual_grad,
    modulated_grad,
    condition,
    modulation,
    norm_gains,
):
    head_width = HEAD_DIM
    row_count = residual.shape[0]
    modulation_all, gains_all = (
        lax.all_gather(modulation, ("seq", "dp"), axis=1, tiled=True),
        lax.all_gather(norm_gains, ("seq", "dp"), axis=1, tiled=True),
    )
    modulated = modulation_all + condition[0]
    query_scale = root_scale(query_raw)
    key_scale = root_scale(key_raw)
    normed_query = (query_raw.astype(jnp.float32) * query_scale * gains_all[0]).astype(jnp.bfloat16)
    normed_key = (key_raw.astype(jnp.float32) * key_scale * gains_all[1]).astype(jnp.bfloat16)
    query_moved, key_moved, value_moved = (
        lax.all_to_all(
            normed_query.reshape(row_count, -1, head_width),
            "seq",
            split_axis=1,
            concat_axis=0,
            tiled=True,
        ),
        lax.all_to_all(
            normed_key.reshape(row_count, -1, head_width),
            "seq",
            split_axis=1,
            concat_axis=0,
            tiled=True,
        ),
        lax.all_to_all(
            values.reshape(row_count, -1, head_width),
            "seq",
            split_axis=1,
            concat_axis=0,
            tiled=True,
        ),
    )
    query_heads = query_moved.transpose(1, 0, 2)
    key_heads = key_moved.transpose(1, 0, 2)
    value_heads = value_moved.transpose(1, 0, 2)
    attended_heads, logsum = lax.map(head_forward, (query_heads, key_heads, value_heads))
    attended_tokens = lax.all_to_all(
        attended_heads.transpose(1, 0, 2), "seq", split_axis=0, concat_axis=1, tiled=True
    )
    attended = attended_tokens.reshape(row_count, -1)
    stream_grad, normed, attended_grad = stream_pass(
        residual, attended, modulated, residual_grad, modulated_grad
    )
    grad_moved = lax.all_to_all(
        attended_grad.reshape(row_count, -1, head_width),
        "seq",
        split_axis=1,
        concat_axis=0,
        tiled=True,
    )
    query_part, key_part, value_part = lax.map(
        head_backward,
        (
            query_heads,
            key_heads,
            value_heads,
            attended_heads,
            grad_moved.transpose(1, 0, 2),
            logsum,
        ),
    )
    query_back, key_back, value_back = (
        lax.all_to_all(
            query_part.transpose(1, 0, 2), "seq", split_axis=0, concat_axis=1, tiled=True
        ),
        lax.all_to_all(key_part.transpose(1, 0, 2), "seq", split_axis=0, concat_axis=1, tiled=True),
        lax.all_to_all(
            value_part.transpose(1, 0, 2), "seq", split_axis=0, concat_axis=1, tiled=True
        ),
    )
    query_grad_n = query_back.reshape(row_count, -1)
    key_grad_n = key_back.reshape(row_count, -1)
    value_sum = value_back.reshape(row_count, -1)
    sums_here = partial_sums(
        attended,
        stream_grad,
        normed,
        modulated_grad,
        query_raw,
        query_scale,
        query_grad_n,
        key_raw,
        key_scale,
        key_grad_n,
    )
    reduced = lax.psum_scatter(sums_here, ("seq", "dp"), scatter_dimension=1, tiled=True)
    factor = (row_count * lax.axis_size("seq") * lax.axis_size("dp")) ** (-0.5)
    return (
        stream_grad.astype(jnp.bfloat16),
        norm_backward(query_raw, query_scale, gains_all[0], query_grad_n),
        norm_backward(key_raw, key_scale, gains_all[1], key_grad_n),
        value_sum.astype(jnp.bfloat16),
        reduced * factor,
    )


def solution(mesh):
    placed = (
        P(("seq", "dp"), None),
        P(("seq", "dp"), None),
        P(("seq", "dp"), None),
        P(("seq", "dp"), None),
        P(("seq", "dp"), None),
        P(("seq", "dp"), None),
        P("dp", None, None),
        P(None, ("seq", "dp")),
        P(None, ("seq", "dp")),
    )
    return jax.shard_map(
        per_device,
        mesh=mesh,
        in_specs=placed,
        out_specs=(
            P(("seq", "dp"), None),
            P(("seq", "dp"), None),
            P(("seq", "dp"), None),
            P(("seq", "dp"), None),
            P(None, ("seq", "dp")),
        ),
        check_vma=False,
    )
```

profile of v0, /device:TPU:1, one launch (start us, length us, event | category | flops | bytes accessed | tf_op | source)
XLA Modules:
  0.0 1958.0 jit_solution(11873094181766818667)
XLA Ops:
  9.8 647.2 %all-gather.1 = f32[256,10,2]{1,2,0:T(2,128)S(1)} all-gather(f32[1,10,2]{1,2,0:T(2,128)S(1)} %bitcast.194), channel_id=1, replica_groups=mesh['seq'=4,'dp'=64] {'seq','dp'}, dimensions={0}, use_global_device_ids=true | all-gather | bytes 20560 | tf_op jit(solution)/shard_map/all_gather | solution.py:125
  691.5 664.9 %all-gather = f32[256,10,2]{1,2,0:T(2,128)S(1)} all-gather(f32[1,10,2]{1,2,0:T(2,128)S(1)} %bitcast.195), channel_id=1, replica_groups=mesh['seq'=4,'dp'=64] {'seq','dp'}, dimensions={0}, use_global_device_ids=true | all-gather | bytes 20560 | tf_op jit(solution)/shard_map/all_gather | solution.py:124
  1368.5 27.5 %while.26 = (s32[]{:T(128)}, bf16[5,768,128]{2,1,0:T(8,128)(2,1)}, f32[5,768]{1,0:T(8,128)}, bf16[5,768,128]{2,1,0:T(8,128)(2,1)}, bf16[5,768,128]{2,1,0:T(8,128...) while((s32[]{:T(128)}, bf16[5,768,128]{2,1,0:T(8,128)(2,1)}, f32[5,768]{1,0:T(8,128)}, ...), condition=%wide.region_5.6_spmd, body=%wide.region_2.5_spmd.sunk | while | flops 306806016 | bytes 7900257 | solution.py:158
  1403.9 19.2 all-to-all-done.3
  1443.0 12.9 all-to-all-done.4
  1457.1 218.5 %while.27 = (s32[]{:T(128)}, f32[5,768,128]{2,0,1:T(8,128)}, f32[5,768,128]{2,0,1:T(8,128)}, bf16[5,768,128]{2,0,1:T(8,128)(2,1)}, bf16[5,768,128]{2,1,0:T(8,128...) while((s32[]{:T(128)}, f32[5,768,128]{2,0,1:T(8,128)}, ...), condition=%wide.region_12.13_spmd, body=%wide.region_10.12_spmd.sunk | while | flops 760675584 | bytes 15945885 | solution.py:173
  1466.9 11.0 dynamic_update_slice.28
  1477.9 11.4 dynamic_update_slice.27
  1489.3 11.4 dynamic_update_slice.26
  1510.6 11.0 dynamic_update_slice.28
  1521.6 11.4 dynamic_update_slice.27
  1533.0 11.4 dynamic_update_slice.26
  1554.3 11.0 dynamic_update_slice.28
  1565.3 11.4 dynamic_update_slice.27
  1576.7 11.4 dynamic_update_slice.26
  1598.0 11.0 dynamic_update_slice.28
  1609.0 11.4 dynamic_update_slice.27
  1620.4 11.4 dynamic_update_slice.26
  1652.7 11.4 dynamic_update_slice.27
  1664.1 11.4 dynamic_update_slice.26
  1675.5 24.6 %all_to_all.120 = bf16[768,5,128]{2,1,0:T(8,128)(2,1)} all-to-all(bf16[768,5,128]{2,1,0:T(8,128)(2,1)} %bitcast.192), channel_id=1, replica_groups=mesh['seq'=4,'dp'=64] {'seq'}, dimensions={0} | all-to-all | bytes 1966080 | tf_op jit(solution)/shard_map/all_to_all | solution.py:189
  1700.1 40.3 %all_to_all.121 = f32[768,5,128]{2,1,0:T(8,128)} all-to-all(f32[768,5,128]{2,1,0:T(8,128)S(1)} %bitcast.191), channel_id=1, replica_groups=mesh['seq'=4,'dp'=64] {'seq'}, dimensions={0} | all-to-all | bytes 3932160 | tf_op jit(solution)/shard_map/all_to_all | solution.py:185
  1756.7 25.5 %all-to-all-done.6 = f32[768,5,128]{2,1,0:T(8,128)} async-done(((f32[768,5,128]{2,1,0:T(8,128)}), f32[768,5,128]{2,1,0:T(8,128)}, u32[]{:S(2)}, u32[]{:S(2)}) %all-to-all-start.6) | async-done | bytes 1966112 | tf_op jit(solution)/shard_map/all_to_all | solution.py:188
  1800.0 157.2 %all-reduce = f32[5,2560]{1,0:T(8,128)S(1)} all-reduce(f32[5,2560]{1,0:T(8,128)S(1)} %stack.23), channel_id=2, replica_groups=mesh['seq'=4,'dp'=64] {'seq','dp'}, use_global_device_ids=true, to_apply=%region_20.21.clone | all-reduce | flops 12800 | bytes 102400
  (176 shorter events, 206.9 us)
Async XLA Ops:
  0.6 9.1 copy-start.18
  0.7 656.6 %copy-start.9 = (bf16[192,2560]{1,0:T(8,128)(2,1)S(1)}, bf16[192,2560]{1,0:T(8,128)(2,1)}, u32[]{:S(2)}) copy-start(bf16[192,2560]{1,0:T(8,128)(2,1)} %param.14) | copy-start | bytes 2949124
  3.0 666.3 %all-to-all-start.2 = ((bf16[192,20,128]{2,0,1:T(8,128)(2,1)}), bf16[192,20,128]{2,0,1:T(8,128)(2,1)S(1)}, u32[]{:S(2)}, u32[]{:S(2)}) async-start(bf16[192,20,128]{2,0,1:T(8,128)(2,1)} %copy_bitcast_fusion.1), calls=%async_computation.2 | async-start | bytes 1966080 | tf_op jit(solution)/shard_map/all_to_all | solution.py:147
  657.2 6.3 copy-start.10
  663.5 3.5 copy-start.14
  669.4 17.1 all-to-all-start.1
  673.5 18.0 copy-start.19
  686.4 679.9 %all-to-all-start = ((bf16[192,20,128]{2,0,1:T(8,128)(2,1)}), bf16[192,20,128]{2,0,1:T(8,128)(2,1)}, u32[]{:S(2)}, u32[]{:S(2)}) async-start(bf16[192,20,128]{2,0,1:T(8,128)(2,1)} %copy.75), calls=%async_computation | async-start | bytes 1966080 | tf_op jit(solution)/shard_map/all_to_all | solution.py:133
  1396.0 7.8 copy-start.12
  1396.0 7.8 copy-start.13
  1399.1 24.0 %all-to-all-start.3 = ((bf16[768,5,128]{2,1,0:T(8,128)(2,1)}), bf16[768,5,128]{2,1,0:T(8,128)(2,1)}, u32[]{:S(2)}, u32[]{:S(2)}) async-start(bf16[768,5,128]{2,1,0:T(8,128)(2,1)} %bitcast.181), calls=%async_computation.3 | async-start | bytes 3145728 | tf_op jit(solution)/shard_map/all_to_all | solution.py:159
  1429.2 3.0 copy-start.5
  1429.2 3.0 copy-start.7
  1438.7 17.2 all-to-all-start.4
  1675.5 24.6 %copy-start.8 = (f32[5,768,128]{2,0,1:T(8,128)S(1)}, f32[5,768,128]{2,0,1:T(8,128)}, u32[]{:S(2)}) copy-start(f32[5,768,128]{2,0,1:T(8,128)} %get-tuple-element.94) | copy-start | bytes 5898244
  1740.4 41.8 %all-to-all-start.6 = ((f32[768,5,128]{2,1,0:T(8,128)}), f32[768,5,128]{2,1,0:T(8,128)}, u32[]{:S(2)}, u32[]{:S(2)}) async-start(f32[768,5,128]{2,1,0:T(8,128)} %bitcast.190), calls=%async_computation.6 | async-start | bytes 6291456 | tf_op jit(solution)/shard_map/all_to_all | solution.py:188
  1782.2 3.4 copy-start.11
  1782.2 3.4 copy-start.15
  1785.6 3.4 copy-start.2
  1785.6 3.4 copy-start.4
  1785.6 3.4 copy-start.17
  1790.6 5.3 copy-start.16
  1793.0 3.0 copy-start.3
  1795.9 162.0 %copy-start.1 = (bf16[192,2560]{1,0:T(8,128)(2,1)S(1)}, bf16[192,2560]{1,0:T(8,128)(2,1)}, u32[]{:S(2)}) copy-start(bf16[192,2560]{1,0:T(8,128)(2,1)} %param.16) | copy-start | bytes 2949124
  (2 other events, 2.5 us)
where the time goes:
time: 1960 us
  blocking collectives  1530 us (78%)
  local copies, waits for them, and re-layouts  232 us (12%)
  waiting for transfers between devices  68.1 us (3%)
  matrix products  57.8 us (3%)
  other arithmetic  34.3 us (2%)
  starting transfers between devices  30.7 us (2%)
    all_gather x1, blocking collectives, per_device(): lax.all_gather(modulation, ('seq', 'dp'), axis=1, tiled=True)  665 us
    all_gather x1, blocking collectives, per_device(): lax.all_gather(norm_gains, ('seq', 'dp'), axis=1, tiled=True)  647 us
    dynamic_update_slice x15, local copies, waits for them, and re-layouts, per_device(): lax.map(head_backward, (query_heads, key_heads, value_heads, attended_hea...  169 us
    unnamed x1, blocking collectives  157 us
    all_to_all x1, blocking collectives, per_device(): lax.all_to_all(query_part.transpose(1, 0, 2), 'seq', split_axis=0, concat...  40.3 us
  transfers between devices with their start and end apart: 6, of which 4 were waited for; matrix products, arithmetic and copies ran while one was open for 2% of the time, Pallas kernels for 0%

commit v1 on v0

--- a/solution.py
+++ b/solution.py
@@ -182,8 +182,14 @@
         ),
     )
     query_back, key_back, value_back = (
-        lax.all_to_all(
-            query_part.transpose(1, 0, 2), "seq", split_axis=0, concat_axis=1, tiled=True
+        jnp.concatenate(
+            lax.all_to_all(
+                jnp.stack(jnp.split(query_part.transpose(1, 0, 2), lax.axis_size("seq"), axis=0)),
+                "seq",
+                0,
+                0,
+            ),
+            axis=1,
         ),
         lax.all_to_all(key_part.transpose(1, 0, 2), "seq", split_axis=0, concat_axis=1, tiled=True),
         lax.all_to_all(

time: 1960 us -> 1880 us (0.959)
  local copies, waits for them, and re-layouts: 232 us -> 175 us
  blocking collectives: 1530 us -> 1490 us
    dynamic_update_slice x15 -> x10, local copies, waits for them, and re-layouts: 169 us -> 112 us  [per_device(): lax.map(head_backward, (query_heads, key_heads, value_heads, attended_hea...]
    all_to_all x1 -> x0, blocking collectives: 40.3 us -> none  [per_device(): lax.all_to_all(query_part.transpose(1, 0, 2), 'seq', split_axis=0, concat...]
  transfers between devices with their start and end apart: 6 -> 7, of which waited for: 4 -> 5; matrix products, arithmetic and copies ran while one was open for 2% -> 2% of each run, Pallas kernels for 0% -> 0%
where the time goes in v1:
time: 1880 us
  blocking collectives  1490 us (79%)
  local copies, waits for them, and re-layouts  175 us (9%)
  waiting for transfers between devices  81.1 us (4%)
  matrix products  56.5 us (3%)
  starting transfers between devices  36 us (2%)
  other arithmetic  35.2 us (2%)
    all_gather x1, blocking collectives, per_device(): lax.all_gather(modulation, ('seq', 'dp'), axis=1, tiled=True)  665 us
    all_gather x1, blocking collectives, per_device(): lax.all_gather(norm_gains, ('seq', 'dp'), axis=1, tiled=True)  647 us
    unnamed x1, blocking collectives  157 us
    dynamic_update_slice x10, local copies, waits for them, and re-layouts, per_device(): lax.map(head_backward, (query_heads, key_heads, value_heads, attended_hea...  112 us
  transfers between devices with their start and end apart: 7, of which 5 were waited for; matrix products, arithmetic and copies ran while one was open for 2% of the time, Pallas kernels for 0%

profile of v1, /device:TPU:1, one launch (start us, length us, event | category | flops | bytes accessed | tf_op | source)
XLA Modules:
  0.0 1878.6 jit_solution(9503832808242437518)
XLA Ops:
  3.0 6.7 all-to-all-start.2
  9.8 647.2 %all-gather.1 = f32[256,10,2]{1,2,0:T(2,128)S(1)} all-gather(f32[1,10,2]{1,2,0:T(2,128)S(1)} %bitcast.199), channel_id=1, replica_groups=mesh['seq'=4,'dp'=64] {'seq','dp'}, dimensions={0}, use_global_device_ids=true | all-gather | bytes 20560 | tf_op jit(solution)/shard_map/all_gather | solution.py:125
  675.9 10.5 all-to-all-done.1
  691.5 664.9 %all-gather = f32[256,10,2]{1,2,0:T(2,128)S(1)} all-gather(f32[1,10,2]{1,2,0:T(2,128)S(1)} %bitcast.200), channel_id=1, replica_groups=mesh['seq'=4,'dp'=64] {'seq','dp'}, dimensions={0}, use_global_device_ids=true | all-gather | bytes 20560 | tf_op jit(solution)/shard_map/all_gather | solution.py:124
  1368.5 27.5 %while.26 = (s32[]{:T(128)}, bf16[5,768,128]{2,1,0:T(8,128)(2,1)}, f32[5,768]{1,0:T(8,128)}, bf16[5,768,128]{2,1,0:T(8,128)(2,1)}, bf16[5,768,128]{2,1,0:T(8,128...) while((s32[]{:T(128)}, bf16[5,768,128]{2,1,0:T(8,128)(2,1)}, f32[5,768]{1,0:T(8,128)}, ...), condition=%wide.region_5.6_spmd, body=%wide.region_2.5_spmd.sunk | while | flops 306806016 | bytes 7900257 | solution.py:158
  1403.9 19.2 %all-to-all-done.3 = bf16[768,5,128]{2,1,0:T(8,128)(2,1)} async-done(((bf16[768,5,128]{2,1,0:T(8,128)(2,1)}), bf16[768,5,128]{2,1,0:T(8,128)(2,1)}, u32[]{:S(2)}, u32[]{:S(2)}) %all-to-all-start.3) | async-done | bytes 983072 | tf_op jit(solution)/shard_map/all_to_all | solution.py:159
  1442.9 12.9 all-to-all-done.4
  1455.9 159.6 %while.27 = (s32[]{:T(128)}, f32[5,768,128]{2,1,0:T(8,128)}, f32[5,768,128]{2,0,1:T(8,128)}, bf16[5,768,128]{2,0,1:T(8,128)(2,1)}, bf16[5,768,128]{2,1,0:T(8,128...) while((s32[]{:T(128)}, f32[5,768,128]{2,1,0:T(8,128)}, ...), condition=%wide.region_12.13_spmd, body=%wide.region_10.12_spmd.sunk | while | flops 760675584 | bytes 15163541 | solution.py:173
  1465.4 11.0 dynamic_update_slice.29
  1476.4 11.4 dynamic_update_slice.28
  1497.4 11.0 dynamic_update_slice.29
  1508.3 11.4 dynamic_update_slice.28
  1529.3 11.0 dynamic_update_slice.29
  1540.3 11.4 dynamic_update_slice.28
  1561.2 11.0 dynamic_update_slice.29
  1572.2 11.4 dynamic_update_slice.28
  1593.1 11.0 dynamic_update_slice.29
  1604.1 11.4 dynamic_update_slice.28
  1615.5 24.3 %all_to_all.110 = bf16[768,5,128]{2,1,0:T(8,128)(2,1)} all-to-all(bf16[768,5,128]{2,1,0:T(8,128)(2,1)} %bitcast.197), channel_id=1, replica_groups=mesh['seq'=4,'dp'=64] {'seq'}, dimensions={0} | all-to-all | bytes 1966080 | tf_op jit(solution)/shard_map/all_to_all | solution.py:195
  1639.8 5.7 all-to-all-start.6
  1648.7 33.0 %all-to-all-done.6 = f32[768,5,128]{2,1,0:T(8,128)} async-done(((f32[768,5,128]{2,1,0:T(8,128)}), f32[768,5,128]{2,1,0:T(8,128)}, u32[]{:S(2)}, u32[]{:S(2)}) %all-to-all-start.6) | async-done | bytes 1966112 | tf_op jit(solution)/shard_map/all_to_all | solution.py:194
  1681.7 5.3 all-to-all-start.5
  1705.1 5.4 all-to-all-done.5
  1720.7 157.3 %all-reduce = f32[5,2560]{1,0:T(8,128)S(1)} all-reduce(f32[5,2560]{1,0:T(8,128)S(1)} %stack.43), channel_id=2, replica_groups=mesh['seq'=4,'dp'=64] {'seq','dp'}, use_global_device_ids=true, to_apply=%region_20.21.clone | all-reduce | flops 12800 | bytes 102400
  (172 shorter events, 173.1 us)
Async XLA Ops:
  0.6 9.1 copy-start.17
  0.7 656.6 %copy-start.8 = (bf16[192,2560]{1,0:T(8,128)(2,1)S(1)}, bf16[192,2560]{1,0:T(8,128)(2,1)}, u32[]{:S(2)}) copy-start(bf16[192,2560]{1,0:T(8,128)(2,1)} %param.14) | copy-start | bytes 2949124
  3.0 666.3 %all-to-all-start.2 = ((bf16[192,20,128]{2,0,1:T(8,128)(2,1)}), bf16[192,20,128]{2,0,1:T(8,128)(2,1)S(1)}, u32[]{:S(2)}, u32[]{:S(2)}) async-start(bf16[192,20,128]{2,0,1:T(8,128)(2,1)} %copy_bitcast_fusion.1), calls=%async_computation.2 | async-start | bytes 1966080 | tf_op jit(solution)/shard_map/all_to_all | solution.py:147
  657.2 6.2 copy-start.9
  663.5 3.5 copy-start.13
  669.3 17.1 all-to-all-start.1
  673.5 18.0 copy-start.18
  686.4 679.9 %all-to-all-start = ((bf16[192,20,128]{2,0,1:T(8,128)(2,1)}), bf16[192,20,128]{2,0,1:T(8,128)(2,1)}, u32[]{:S(2)}, u32[]{:S(2)}) async-start(bf16[192,20,128]{2,0,1:T(8,128)(2,1)} %copy.75), calls=%async_computation | async-start | bytes 1966080 | tf_op jit(solution)/shard_map/all_to_all | solution.py:133
  1396.0 7.9 copy-start.11
  1396.0 7.9 copy-start.12
  1399.1 24.1 %all-to-all-start.3 = ((bf16[768,5,128]{2,1,0:T(8,128)(2,1)}), bf16[768,5,128]{2,1,0:T(8,128)(2,1)}, u32[]{:S(2)}, u32[]{:S(2)}) async-start(bf16[768,5,128]{2,1,0:T(8,128)(2,1)} %bitcast.187), calls=%async_computation.3 | async-start | bytes 3145728 | tf_op jit(solution)/shard_map/all_to_all | solution.py:159
  1429.2 3.0 copy-start.5
  1429.2 3.0 copy-start.7
  1438.6 17.2 all-to-all-start.4
  1639.8 41.9 %all-to-all-start.6 = ((f32[768,5,128]{2,1,0:T(8,128)}), f32[768,5,128]{2,1,0:T(8,128)}, u32[]{:S(2)}, u32[]{:S(2)}) async-start(f32[768,5,128]{2,1,0:T(8,128)} %bitcast.196), calls=%async_computation.6 | async-start | bytes 6291456 | tf_op jit(solution)/shard_map/all_to_all | solution.py:194
  1681.7 28.8 %all-to-all-start.5 = ((f32[4,192,5,128]{3,1,2,0:T(8,128)}), f32[4,192,5,128]{3,1,2,0:T(8,128)}, u32[]{:S(2)}, u32[]{:S(2)}) async-start(f32[4,192,5,128]{3,1,2,0:T(8,128)} %pad_maximum_fusion), calls=%async_computation.5 | async-start | bytes 3932160 | tf_op jit(solution)/shard_map/all_to_all | solution.py:186
  1694.3 3.4 copy-start.10
  1694.3 3.4 copy-start.14
  1697.7 3.4 copy-start.2
  1697.7 3.4 copy-start.3
  1697.8 3.4 copy-start.16
  1713.6 3.0 copy-start.4
  1713.6 3.0 copy-start.15
  1716.6 162.0 %copy-start.1 = (bf16[192,2560]{1,0:T(8,128)(2,1)S(1)}, bf16[192,2560]{1,0:T(8,128)(2,1)}, u32[]{:S(2)}) copy-start(bf16[192,2560]{1,0:T(8,128)(2,1)} %param.16) | copy-start | bytes 2949124
  (2 other events, 2.5 us)
